TPU v7x, 512 devices: a whole 4x4x16 slice. The times are simulated.
512 devices in a mesh: gx: 32 (over z_lo, y, core), gy: 16 (over x, z_hi).
Axes of the slice: x: 4, y: 4, z: 16 (z_hi: 4, z_lo: 4; z = z_hi * 4 + z_lo), core: 2. Of those that a mesh axis runs over, the one named last changes fastest.
Arguments:
- deflation: float32 [32, 320, 80, 128], P(None, 'gx', 'gy'), may hold values from -13 to 13
- layers: int32 [256, 48, 128], P('gx', 'gy'), may hold values from 0 to 84
- layer_table: float32 [85], replicated, may hold values from 0.02 to 2
- forcing: float32 [256, 48, 128], P('gx', 'gy'), may hold values from -13 to 13
Outputs:
- coarse_rows: float32 [32, 16, 9, 32, 32], P('gx', 'gy')
- coarse_solution: float32 [32, 16, 32], P('gx', 'gy')
All inputs are finite; a program needn't handle non-finite values.
Results may differ from a plain program's by a relative error of at most 0.0003.
Values sent between devices are 32-bit elements; how exact they have to be, the bound alone decides.
A program may use at most 64 MiB of HBM per device.

v0:
```python
import math
import jax
import jax.numpy as jnp
from jax import lax
from jax.sharding import PartitionSpec as P

VEC = 32
CX = 8
CY = 3
CZ = 128
MARGIN = 1
LAYERS = 85
ITERS = 3
EX = 10
EY = 5
storage_term = 0.5
upper_offsets = ((0, 0), (0, 1), (1, -1), (1, 0), (1, 1))


def extended(value, sides, width):
    for axis, dim in sides:
        devices, length = (lax.axis_size(axis), value.shape[dim])
        up = [(i, (i + 1) % devices) for i in range(devices - 1)]
        down = [(j, i) for i, j in up]
        last = lax.slice_in_dim(value, length - width, length, axis=dim)
        initial = lax.slice_in_dim(value, 0, width, axis=dim)
        before = lax.ppermute(last, axis, up)
        after = lax.ppermute(initial, axis, down)
        value = jnp.concatenate([before, value, after], axis=dim)
    return value


def unity_weights(index_pos, subdomains, own_cells):
    offset = jnp.arange(own_cells + 2 * MARGIN, dtype=jnp.int32)
    global_pos = index_pos * own_cells - MARGIN + offset
    inside = ((global_pos >= 0) & (global_pos < subdomains * own_cells)).astype(jnp.float32)
    below_side = ((index_pos > 0) & (global_pos < index_pos * own_cells + MARGIN)).astype(
        jnp.float32
    )
    above_side = (
        (index_pos < subdomains - 1) & (global_pos >= (index_pos + 1) * own_cells - MARGIN)
    ).astype(jnp.float32)
    return inside / (1.0 + below_side + above_side)


def operate(padded, kappa_box):
    centre = padded[:, 1:-1, 1:-1]
    kappa_centre = kappa_box[1:-1, 1:-1]
    width_x = centre.shape[1]
    width_y = centre.shape[2]
    result = storage_term * centre
    for shift_x, shift_y in ((1, 0), (-1, 0), (0, 1), (0, -1)):
        beside = padded[:, 1 + shift_x : 1 + shift_x + width_x, 1 + shift_y : 1 + shift_y + width_y]
        kappa_beside = kappa_box[
            1 + shift_x : 1 + shift_x + width_x, 1 + shift_y : 1 + shift_y + width_y
        ]
        result = result + jnp.sqrt(kappa_centre * kappa_beside) * (centre - beside)
    for forward in (True, False):
        if forward:
            beside = jnp.pad(centre[..., 1:], ((0, 0), (0, 0), (0, 0), (0, 1)))
            kappa_beside = jnp.pad(kappa_centre[..., 1:], ((0, 0), (0, 0), (0, 1)))
        else:
            beside = jnp.pad(centre[..., :-1], ((0, 0), (0, 0), (0, 0), (1, 0)))
            kappa_beside = jnp.pad(kappa_centre[..., :-1], ((0, 0), (0, 0), (1, 0)))
        result = result + jnp.sqrt(kappa_centre * kappa_beside) * (centre - beside)
    return result


def strip_bounds(shift, ext_cells):
    slab_depth = 2 * MARGIN + 1
    if shift < 0:
        return (0, 0, slab_depth)
    if shift == 0:
        return (slab_depth, 1, ext_cells)
    return (slab_depth + ext_cells, ext_cells + 2 - slab_depth, slab_depth)


def block_with(applied, strip, shift_x, shift_y):
    unused_x, start_bx, length_x = strip_bounds(shift_x, EX)
    unused_y, start_by, length_y = strip_bounds(shift_y, EY)
    region = applied[:, start_bx : start_bx + length_x, start_by : start_by + length_y]
    return jnp.dot(
        region.reshape(VEC, -1), strip.reshape(VEC, -1).T, precision=lax.Precision.HIGHEST
    )


def conjugate(coarse_load, image_of, total_of):
    solution = jnp.zeros_like(coarse_load)
    residual = coarse_load
    direction = coarse_load
    norm_now = total_of(jnp.sum(residual * residual))
    for iteration in range(ITERS):
        mapped = image_of(direction)
        step_size = norm_now / total_of(jnp.sum(direction * mapped))
        solution = solution + step_size * direction
        residual = residual - step_size * mapped
        norm_next = total_of(jnp.sum(residual * residual))
        direction = residual + norm_next / norm_now * direction
        norm_now = norm_next
    return solution


def plain_total(value):
    return value


def take_from(vector, offset, reach):
    count = vector.shape[1]
    padded_vec = jnp.pad(vector, ((0, 0), (reach, reach)))
    return padded_vec[:, reach + offset : reach + offset + count]


def half_product(upper_rows, vector, mesh_x, mesh_y):
    count = vector.shape[1]
    reach = mesh_y + 1
    flat = jnp.arange(count, dtype=jnp.int32)
    place_x = flat // mesh_y
    place_y = flat % mesh_y
    result = jnp.zeros_like(vector)
    spread = jnp.zeros_like(vector)
    for slot_index in range(len(upper_offsets)):
        shift_x, shift_y = upper_offsets[slot_index]
        offset = shift_x * mesh_y + shift_y
        valid = (
            (place_x + shift_x >= 0)
            & (place_x + shift_x < mesh_x)
            & (place_y + shift_y >= 0)
            & (place_y + shift_y < mesh_y)
        ).astype(jnp.float32)
        coarse_block = upper_rows[slot_index]
        moved = take_from(vector, offset, reach) * valid[None, :]
        result = result + jnp.sum(coarse_block * moved[None, :, :], axis=1)
        if shift_x != 0 or shift_y != 0:
            sent_back = jnp.sum(coarse_block * vector[:, None, :], axis=0) * valid[None, :]
            spread = spread + take_from(sent_back, -offset, reach)
    return result + spread


def body(deflation, layers, layer_table, forcing):
    mesh_x = lax.axis_size("gx")
    mesh_y = lax.axis_size("gy")
    index_x = lax.axis_index("gx")
    index_y = lax.axis_index("gy")
    slab_depth = 2 * MARGIN + 1
    onehot = (layers.reshape(1, -1) == jnp.arange(LAYERS, dtype=jnp.int32)[:, None]).astype(
        jnp.float32
    )
    permeability = jnp.dot(layer_table, onehot, precision=lax.Precision.HIGHEST).reshape(CX, CY, CZ)
    fields = jnp.stack([permeability, forcing])
    rimmed = extended(fields, (("gx", 1), ("gy", 2)), MARGIN + 1)
    weights = (
        unity_weights(index_x, mesh_x, CX)[:, None, None]
        * unity_weights(index_y, mesh_y, CY)[None, :, None]
    )
    basis = deflation * weights * (1.0 / math.sqrt(CX * CY * CZ))
    kappa_box = jnp.pad(rimmed[0], ((1, 1), (1, 1), (0, 0)))
    forcing_ext = rimmed[1, 1:-1, 1:-1]
    applied = operate(jnp.pad(basis, ((0, 0), (2, 2), (2, 2), (0, 0))), kappa_box)
    coarse_load = jnp.dot(
        basis.reshape(VEC, -1), forcing_ext.reshape(-1), precision=lax.Precision.HIGHEST
    )
    beside_all = extended(basis, (("gx", 1), ("gy", 2)), slab_depth)
    blocks = []
    for shift_x in (-1, 0, 1):
        for shift_y in (-1, 0, 1):
            start_nx, unused_bx, length_x = strip_bounds(shift_x, EX)
            start_ny, unused_by, length_y = strip_bounds(shift_y, EY)
            strip = beside_all[:, start_nx : start_nx + length_x, start_ny : start_ny + length_y]
            blocks.append(block_with(applied, strip, shift_x, shift_y))
    coarse_rows = jnp.stack(blocks)
    gathered_rows, gathered_load = (
        lax.all_gather(coarse_rows[4:].reshape(1, 5 * VEC * VEC), ("gx", "gy"), axis=0, tiled=True),
        lax.all_gather(coarse_load.reshape(1, VEC), ("gx", "gy"), axis=0, tiled=True),
    )
    upper_rows = gathered_rows.T.reshape(5, VEC, VEC, mesh_x * mesh_y)
    whole_load = gathered_load.T

    def image_all(vector):
        return half_product(upper_rows, vector, mesh_x, mesh_y)

    whole_solution = conjugate(whole_load, image_all, plain_total)
    flat_index = index_x * mesh_y + index_y
    solution = lax.dynamic_slice(whole_solution, (jnp.int32(0), flat_index), (VEC, 1)).reshape(
        1, 1, VEC
    )
    return (coarse_rows[None, None], solution)


def solution(mesh):
    return jax.shard_map(
        body,
        mesh=mesh,
        in_specs=(P(None, "gx", "gy", None), P("gx", "gy", None), P(), P("gx", "gy", None)),
        out_specs=(P("gx", "gy", None, None, None), P("gx", "gy", None)),
        check_vma=False,
    )
```

profile of v0, /device:TPU:99, one launch (start us, length us, event | category | flops | bytes accessed | tf_op | source)
XLA Modules:
  0.0 2032.0 jit_solution(9259440537845964551)
XLA Ops:
  7.2 0.7 copy.54
  7.9 0.7 copy.39
  8.7 0.5 fusion.18
  9.2 2.6 collective-permute-start.1
  11.7 3.1 collective-permute-start
  15.0 1.3 multiply_multiply_fusion
  16.3 0.8 fusion.85
  17.1 2.7 collective-permute-start.5
  19.8 2.8 collective-permute-start.4
  22.7 0.6 fusion.87
  23.4 9.7 collective-permute-start.3
  33.1 1.9 collective-permute-start.2
  35.0 1.5 pad_slice_fusion.1
  36.5 0.5 copy.41
  37.1 1.2 reshape.203
  38.2 4.6 collective-permute-done.2
  42.8 0.7 pad_maximum_fusion.3
  43.6 1.9 convolution_bitcast_fusion.9
  45.5 0.3 dynamic-update-slice
  45.8 0.6 copy-done.5
  46.5 0.8 pad_maximum_fusion.1
  47.3 1.2 pad_maximum_fusion
  48.5 0.2 fusion.84
  48.7 2.1 collective-permute-start.6
  50.8 0.1 fusion.86
  50.9 0.1 fusion.53
  51.0 8.2 collective-permute-start.7
  59.2 1.1 fusion.7
  60.3 64.6 %collective-permute-done.6 = f32[32,16,3,128]{3,0,2,1:T(8,128)S(1)} collective-permute-done((f32[32,16,3,128]{3,0,2,1:T(8,128)S(1)}, f32[32,16,3,128]{3,0,2,1:T(8,128)S(1)}, u32[]{:S(2)}, u32[]{:S(2)}) %collective-permute-start.6) | collective-permute-done | bytes 786464 | tf_op jit(solution)/shard_map/ppermute | solution.py:27
  124.9 0.3 fusion.17
  125.1 1.3 fusion.16
  126.4 0.3 fusion.15
  126.7 0.5 fusion.14
  127.2 0.8 constant_dynamic-update-slice_fusion.9
  128.0 0.5 constant_dynamic-update-slice_fusion.8
  128.6 0.3 constant_dynamic-update-slice_fusion.7
  128.9 1.3 constant_dynamic-update-slice_fusion.6
  130.2 0.3 constant_dynamic-update-slice_fusion.5
  130.5 0.7 reshape.210
  131.2 402.9 %all-reduce.24.cloned.1.call-done = f32[16384]{0:T(1024)} async-done(((f32[16384]{0:T(1024)}), f32[16384]{0:T(1024)}) %all-reduce.24.cloned.1.call-update) | async-done | bytes 65552
  534.2 0.9 reshape.207
  535.1 0.1 copy.42
  535.3 1425.0 %all-gather.4.cloned.1.call-done = f32[512,1,5120]{2,1,0:T(1,128)} async-done(((f32[1,1,5120]{2,1,0:T(1,128)}), f32[512,1,5120]{2,1,0:T(1,128)}) %all-gather.4.cloned.1.call-update) | async-done | bytes 10485776 | tf_op jit(solution)/shard_map/all_gather | solution.py:172
  1960.3 22.0 %copy.43 = f32[512,1,5120]{0,2,1:T(8,128)} copy(f32[512,1,5120]{2,1,0:T(1,128)} %all-gather.4.cloned.1.call-done) | data formatting | bytes 20971520 | tf_op jit(solution)/shard_map/all_gather | solution.py:172
  1982.3 4.7 fusion.83
  1987.0 1.1 multiply_reduce_fusion.18
  1988.1 0.1 copy-done.1
  1988.3 0.8 copy-done.2
  1989.1 1.0 copy-done.3
  1990.1 0.1 fusion.43
  1990.3 1.3 slice-done.2
  1991.5 2.1 multiply_reduce_fusion.25
  1993.7 0.7 multiply_reduce_fusion.30
  1995.7 0.6 multiply_reduce_fusion.29
  1997.6 4.1 multiply_reduce_fusion.9
  2001.6 0.1 fusion.47
  2001.8 6.3 multiply_reduce_fusion.16
  2008.0 0.7 multiply_reduce_fusion.28
  2010.0 0.6 multiply_reduce_fusion.27
  2011.9 4.1 multiply_reduce_fusion
  2016.0 0.1 fusion.51
  2016.1 6.3 multiply_reduce_fusion.7
  2022.4 0.7 fusion.39
  2024.4 0.7 fusion.61
  (44 shorter events, 0.4 us)
Async XLA Ops:
  7.2 1.5 copy-start
  7.2 527.0 %all-reduce.24.cloned.1.call-start = ((), (), s32[]{:S(2)}) async-start(), calls=%async_computation | async-start | bytes 131072
  9.2 13.5 collective-permute-start.1
  11.7 10.9 collective-permute-start
  17.1 30.2 %collective-permute-start.5 = (f32[32,3,5,128]{3,0,2,1:T(8,128)}, f32[32,3,5,128]{3,0,2,1:T(8,128)}, u32[]{:S(2)}, u32[]{:S(2)}) collective-permute-start(f32[32,3,5,128]{3,0,2,1:T(8,128)} %get-tuple-element.47), channel_id=1, source_target_pairs={{16,0},{32,16},{48,32},{64,48},{80,64},{96,80},{112,96},{128,112},... | collective-permute-start | bytes 737288 | tf_op jit(solution)/shard_map/ppermute | solution.py:28
  19.8 27.5 %collective-permute-start.4 = (f32[32,3,5,128]{3,0,2,1:T(8,128)}, f32[32,3,5,128]{3,0,2,1:T(8,128)}, u32[]{:S(2)}, u32[]{:S(2)}) collective-permute-start(f32[32,3,5,128]{3,0,2,1:T(8,128)} %get-tuple-element.46), channel_id=1, source_target_pairs={{0,16},{16,32},{32,48},{48,64},{64,80},{80,96},{96,112},{112,128},... | collective-permute-start | bytes 737288 | tf_op jit(solution)/shard_map/ppermute | solution.py:27
  22.7 10.4 copy-start.6
  23.4 14.9 collective-permute-start.3
  33.1 9.7 collective-permute-start.2
  45.8 0.6 copy-start.5
  46.4 1913.9 %all-gather.4.cloned.1.call-start = ((), (), s32[]{:S(2)}) async-start(), calls=%async_computation.1 | async-start | bytes 10506240 | tf_op jit(solution)/shard_map/all_gather | solution.py:172
  48.5 10.6 copy-start.4
  48.7 76.1 %collective-permute-start.6 = (f32[32,16,3,128]{3,0,2,1:T(8,128)S(1)}, f32[32,16,3,128]{3,0,2,1:T(8,128)S(1)}, u32[]{:S(2)}, u32[]{:S(2)}) collective-permute-start(f32[32,16,3,128]{3,0,2,1:T(8,128)S(1)} %get-tuple-element.45), channel_id=1, source_target_pairs={{0,1},{1,2},{2,3},{3,4},{4,5},{5,6},{6,7},{7,8},{8,9},{9,10},{10,1... | collective-permute-start | bytes 2359304 | tf_op jit(solution)/shard_map/ppermute | solution.py:27
  51.0 75.5 %collective-permute-start.7 = (f32[32,16,3,128]{3,0,2,1:T(8,128)S(1)}, f32[32,16,3,128]{3,0,2,1:T(8,128)S(1)}, u32[]{:S(2)}, u32[]{:S(2)}) collective-permute-start(f32[32,16,3,128]{3,0,2,1:T(8,128)S(1)} %get-tuple-element.44), channel_id=1, source_target_pairs={{1,0},{2,1},{3,2},{4,3},{5,4},{6,5},{7,6},{8,7},{9,8},{10,9},{11,1... | collective-permute-start | bytes 2359304 | tf_op jit(solution)/shard_map/ppermute | solution.py:28
  130.5 1851.8 %copy-start.7 = (f32[9,32,32]{2,1,0:T(8,128)}, f32[9,32,32]{2,1,0:T(8,128)S(1)}, u32[]{:S(2)}) copy-start(f32[9,32,32]{2,1,0:T(8,128)S(1)} %get-tuple-element.75) | copy-start | bytes 110596
  1982.3 8.0 slice-start
  1982.3 8.0 slice-start.1
  1987.0 1.3 copy-start.1
  1987.0 2.1 copy-start.2
  1987.0 3.1 copy-start.3
  1987.0 4.5 slice-start.2
Sparse Core Ops, SparseCore 0:
  46.5 487.5 all-reduce.23
  536.7 1423.5 all-gather.3
where the time goes:
time: 2030 us
  waiting for transfers between devices  1900 us (94%)
  local copies, waits for them, and re-layouts  39 us (2%)
  other arithmetic  33.9 us (2%)
  starting transfers between devices  33.2 us (2%)
  between operations  20.8 us (1%)
    all_gather x1, waiting for transfers between devices, body(): lax.all_gather(coarse_rows[4:].reshape(1, 5 * VEC * VEC), ('gx', 'gy'), a...  1430 us
    unnamed x3, waiting for transfers between devices  403 us
    ppermute x4, waiting for transfers between devices, extended(): before = lax.ppermute(last, axis, up)  69.1 us
  transfers between devices with their start and end apart: 10, of which 4 were waited for; matrix products, arithmetic and copies ran while one was open for 1% of the time, Pallas kernels for 0%

commit v1 on v0

--- a/solution.py
+++ b/solution.py
@@ -168,8 +168,14 @@
             strip = beside_all[:, start_nx : start_nx + length_x, start_ny : start_ny + length_y]
             blocks.append(block_with(applied, strip, shift_x, shift_y))
     coarse_rows = jnp.stack(blocks)
+
+    def switch_record(row_data, mesh_ax):
+        return jnp.concatenate(
+            lax.all_to_all(jnp.stack([row_data] * lax.axis_size(mesh_ax)), mesh_ax, 0, 0), axis=0
+        )
+
     gathered_rows, gathered_load = (
-        lax.all_gather(coarse_rows[4:].reshape(1, 5 * VEC * VEC), ("gx", "gy"), axis=0, tiled=True),
+        switch_record(coarse_rows[4:].reshape(1, 5 * VEC * VEC), ("gx", "gy")),
         lax.all_gather(coarse_load.reshape(1, VEC), ("gx", "gy"), axis=0, tiled=True),
     )
     upper_rows = gathered_rows.T.reshape(5, VEC, VEC, mesh_x * mesh_y)

time: 2030 us -> 780 us (0.38)
  the two profiles are of different devices: /device:TPU:99 before, /device:TPU:1 now
where the time goes in v1:
time: 780 us; the launch traced here: 779 us
  waiting for transfers between devices  624 us (80%)
  starting transfers between devices  56.5 us (7%)
  local copies, waits for them, and re-layouts  41.7 us (5%)
  other arithmetic  31.3 us (4%)
  between operations  20.8 us (3%)
    unnamed x2, waiting for transfers between devices  551 us
    ppermute x4, waiting for transfers between devices, extended(): after = lax.ppermute(initial, axis, down)  47.2 us
    ppermute x4, waiting for transfers between devices, extended(): before = lax.ppermute(last, axis, up)  25.7 us
    all_to_all x1, local copies, waits for them, and re-layouts, switch_record(): lax.all_to_all(jnp.stack([row_data] * lax.axis_size(mesh_ax)), mesh_ax, 0...  22 us
    all_to_all x1, starting transfers between devices, switch_record(): lax.all_to_all(jnp.stack([row_data] * lax.axis_size(mesh_ax)), mesh_ax, 0...  21.7 us
    ppermute x4, starting transfers between devices, extended(): before = lax.ppermute(last, axis, up)  21 us
  transfers between devices with their start and end apart: 10, of which 4 were waited for; matrix products, arithmetic and copies ran while one was open for 1% of the time, Pallas kernels for 0%

profile of v1, /device:TPU:1, one launch (start us, length us, event | category | flops | bytes accessed | tf_op | source)
XLA Modules:
  0.0 779.0 jit_solution(660774061685813022)
XLA Ops:
  7.2 0.7 copy.53
  7.9 0.7 copy.38
  8.6 0.5 fusion.18
  9.1 8.8 %collective-permute-start.1 = (f32[2,2,3,128]{3,2,1,0:T(4,128)S(1)}, f32[2,2,3,128]{3,2,1,0:T(4,128)S(1)}, u32[]{:S(2)}, u32[]{:S(2)}) collective-permute-start(f32[2,2,3,128]{3,2,1,0:T(4,128)S(1)} %get-tuple-element.73), channel_id=1, source_target_pairs={{16,0},{32,16},{48,32},{64,48},{80,64},{96,80},{112,96},{128,112},... | collective-permute-start | bytes 18440 | tf_op jit(solution)/shard_map/ppermute | solution.py:28
  17.9 1.9 collective-permute-start
  19.9 0.1 broadcast_multiply_fusion.15
  20.0 1.3 multiply_multiply_fusion
  21.3 2.4 collective-permute-start.5
  23.7 3.2 collective-permute-start.4
  27.0 1.3 collective-permute-start.3
  28.3 7.9 %collective-permute-start.2 = (f32[2,12,2,128]{3,2,1,0:T(2,128)S(1)}, f32[2,12,2,128]{3,2,1,0:T(2,128)S(1)}, u32[]{:S(2)}, u32[]{:S(2)}) collective-permute-start(f32[2,12,2,128]{3,2,1,0:T(2,128)S(1)} %get-tuple-element.70), channel_id=1, source_target_pairs={{0,1},{1,2},{2,3},{3,4},{4,5},{5,6},{6,7},{7,8},{8,9},{9,10},{10,1... | collective-permute-start | bytes 73736 | tf_op jit(solution)/shard_map/ppermute | solution.py:27
  36.2 0.4 pad_slice_fusion.1
  36.6 0.6 collective-permute-done.2
  37.2 0.1 pad_maximum_fusion
  37.3 0.2 fusion.84
  37.5 8.1 %collective-permute-start.6 = (f32[32,16,3,128]{3,0,2,1:T(8,128)S(1)}, f32[32,16,3,128]{3,0,2,1:T(8,128)S(1)}, u32[]{:S(2)}, u32[]{:S(2)}) collective-permute-start(f32[32,16,3,128]{3,0,2,1:T(8,128)S(1)} %get-tuple-element.45), channel_id=1, source_target_pairs={{0,1},{1,2},{2,3},{3,4},{4,5},{5,6},{6,7},{7,8},{8,9},{9,10},{10,1... | collective-permute-start | bytes 2359304 | tf_op jit(solution)/shard_map/ppermute | solution.py:27
  45.6 0.1 fusion.86
  45.7 0.1 fusion.53
  45.8 1.3 collective-permute-start.7
  47.1 1.1 fusion.7
  48.2 25.2 %collective-permute-done.6 = f32[32,16,3,128]{3,0,2,1:T(8,128)S(1)} collective-permute-done((f32[32,16,3,128]{3,0,2,1:T(8,128)S(1)}, f32[32,16,3,128]{3,0,2,1:T(8,128)S(1)}, u32[]{:S(2)}, u32[]{:S(2)}) %collective-permute-start.6) | collective-permute-done | bytes 786464 | tf_op jit(solution)/shard_map/ppermute | solution.py:27
  73.4 0.3 fusion.17
  73.6 0.4 fusion.16
  74.0 47.2 %collective-permute-done.7 = f32[32,16,3,128]{3,0,2,1:T(8,128)S(1)} collective-permute-done((f32[32,16,3,128]{3,0,2,1:T(8,128)S(1)}, f32[32,16,3,128]{3,0,2,1:T(8,128)S(1)}, u32[]{:S(2)}, u32[]{:S(2)}) %collective-permute-start.7) | collective-permute-done | bytes 786464 | tf_op jit(solution)/shard_map/ppermute | solution.py:28
  121.2 0.3 fusion.15
  121.4 0.5 fusion.14
  122.0 0.8 constant_dynamic-update-slice_fusion.9
  122.8 0.5 constant_dynamic-update-slice_fusion.8
  123.3 0.3 constant_dynamic-update-slice_fusion.7
  123.6 0.4 constant_dynamic-update-slice_fusion.6
  124.0 0.3 constant_dynamic-update-slice_fusion.5
  124.2 0.1 stack_reshape.5
  124.3 6.8 stack.54
  131.1 21.7 %all-to-all-start = ((f32[512,1,5120]{2,1,0:T(1,128)}), f32[512,1,5120]{2,1,0:T(1,128)}, u32[]{:S(2)}, u32[]{:S(2)}) async-start(f32[512,1,5120]{2,1,0:T(1,128)} %stack.54), calls=%async_computation | async-start | bytes 20971520 | tf_op jit(solution)/shard_map/all_to_all | solution.py:174
  152.8 0.0 all-reduce.24.cloned.1.call-start
  152.8 0.5 copy.40
  153.3 0.2 reshape.207
  153.7 0.7 convolution_bitcast_fusion.9
  154.5 0.3 dynamic-update-slice
  154.7 0.6 copy-done.4
  155.4 550.8 %all-reduce.24.cloned.1.call-done = f32[16384]{0:T(1024)} async-done(((f32[16384]{0:T(1024)}), f32[16384]{0:T(1024)}) %all-reduce.24.cloned.1.call-update) | async-done | bytes 65552
  706.2 0.9 reshape.211
  707.1 0.1 copy.41
  707.3 22.0 %copy.42 = f32[512,1,5120]{0,2,1:T(8,128)} copy(f32[512,1,5120]{2,1,0:T(1,128)} %all-to-all-done) | data formatting | bytes 20971520 | tf_op jit(solution)/shard_map/all_to_all | solution.py:174
  729.3 4.7 fusion.83
  734.0 1.1 multiply_reduce_fusion.18
  735.1 0.1 copy-done.1
  735.3 0.8 copy-done.2
  736.1 1.0 copy-done.3
  737.1 0.1 fusion.43
  737.3 1.3 slice-done.2
  738.5 2.1 multiply_reduce_fusion.25
  740.7 0.7 multiply_reduce_fusion.30
  742.7 0.6 multiply_reduce_fusion.29
  744.6 4.1 multiply_reduce_fusion.9
  748.6 0.1 fusion.47
  748.8 6.3 multiply_reduce_fusion.16
  755.0 0.7 multiply_reduce_fusion.28
  757.0 0.6 multiply_reduce_fusion.27
  758.9 4.1 multiply_reduce_fusion
  763.0 0.1 fusion.51
  763.1 6.3 multiply_reduce_fusion.7
  769.4 0.7 fusion.39
  771.4 0.7 fusion.61
  (40 shorter events, 0.4 us)
Async XLA Ops:
  7.2 1.5 copy-start
  9.1 17.8 %collective-permute-start.1 = (f32[2,2,3,128]{3,2,1,0:T(4,128)S(1)}, f32[2,2,3,128]{3,2,1,0:T(4,128)S(1)}, u32[]{:S(2)}, u32[]{:S(2)}) collective-permute-start(f32[2,2,3,128]{3,2,1,0:T(4,128)S(1)} %get-tuple-element.73), channel_id=1, source_target_pairs={{16,0},{32,16},{48,32},{64,48},{80,64},{96,80},{112,96},{128,112},... | collective-permute-start | bytes 18440 | tf_op jit(solution)/shard_map/ppermute | solution.py:28
  17.9 9.0 %collective-permute-start = (f32[2,2,3,128]{3,2,1,0:T(4,128)S(1)}, f32[2,2,3,128]{3,2,1,0:T(4,128)S(1)}, u32[]{:S(2)}, u32[]{:S(2)}) collective-permute-start(f32[2,2,3,128]{3,2,1,0:T(4,128)S(1)} %get-tuple-element.72), channel_id=1, source_target_pairs={{0,16},{16,32},{32,48},{48,64},{64,80},{80,96},{96,112},{112,128},... | collective-permute-start | bytes 18440 | tf_op jit(solution)/shard_map/ppermute | solution.py:27
  21.3 15.9 %collective-permute-start.5 = (f32[32,3,5,128]{3,0,2,1:T(8,128)S(1)}, f32[32,3,5,128]{3,0,2,1:T(8,128)S(1)}, u32[]{:S(2)}, u32[]{:S(2)}) collective-permute-start(f32[32,3,5,128]{3,0,2,1:T(8,128)S(1)} %get-tuple-element.47), channel_id=1, source_target_pairs={{16,0},{32,16},{48,32},{64,48},{80,64},{96,80},{112,96},{128,112},... | collective-permute-start | bytes 737288 | tf_op jit(solution)/shard_map/ppermute | solution.py:28
  23.7 13.5 %collective-permute-start.4 = (f32[32,3,5,128]{3,0,2,1:T(8,128)S(1)}, f32[32,3,5,128]{3,0,2,1:T(8,128)S(1)}, u32[]{:S(2)}, u32[]{:S(2)}) collective-permute-start(f32[32,3,5,128]{3,0,2,1:T(8,128)S(1)} %get-tuple-element.46), channel_id=1, source_target_pairs={{0,16},{16,32},{32,48},{48,64},{64,80},{80,96},{96,112},{112,128},... | collective-permute-start | bytes 737288 | tf_op jit(solution)/shard_map/ppermute | solution.py:27
  27.0 9.6 %collective-permute-start.3 = (f32[2,12,2,128]{3,2,1,0:T(2,128)S(1)}, f32[2,12,2,128]{3,2,1,0:T(2,128)S(1)}, u32[]{:S(2)}, u32[]{:S(2)}) collective-permute-start(f32[2,12,2,128]{3,2,1,0:T(2,128)S(1)} %get-tuple-element.71), channel_id=1, source_target_pairs={{1,0},{2,1},{3,2},{4,3},{5,4},{6,5},{7,6},{8,7},{9,8},{10,9},{11,1... | collective-permute-start | bytes 73736 | tf_op jit(solution)/shard_map/ppermute | solution.py:28
  28.3 8.9 %collective-permute-start.2 = (f32[2,12,2,128]{3,2,1,0:T(2,128)S(1)}, f32[2,12,2,128]{3,2,1,0:T(2,128)S(1)}, u32[]{:S(2)}, u32[]{:S(2)}) collective-permute-start(f32[2,12,2,128]{3,2,1,0:T(2,128)S(1)} %get-tuple-element.70), channel_id=1, source_target_pairs={{0,1},{1,2},{2,3},{3,4},{4,5},{5,6},{6,7},{7,8},{8,9},{9,10},{10,1... | collective-permute-start | bytes 73736 | tf_op jit(solution)/shard_map/ppermute | solution.py:27
  37.5 35.8 %collective-permute-start.6 = (f32[32,16,3,128]{3,0,2,1:T(8,128)S(1)}, f32[32,16,3,128]{3,0,2,1:T(8,128)S(1)}, u32[]{:S(2)}, u32[]{:S(2)}) collective-permute-start(f32[32,16,3,128]{3,0,2,1:T(8,128)S(1)} %get-tuple-element.45), channel_id=1, source_target_pairs={{0,1},{1,2},{2,3},{3,4},{4,5},{5,6},{6,7},{7,8},{8,9},{9,10},{10,1... | collective-permute-start | bytes 2359304 | tf_op jit(solution)/shard_map/ppermute | solution.py:27
  45.8 75.4 %collective-permute-start.7 = (f32[32,16,3,128]{3,0,2,1:T(8,128)S(1)}, f32[32,16,3,128]{3,0,2,1:T(8,128)S(1)}, u32[]{:S(2)}, u32[]{:S(2)}) collective-permute-start(f32[32,16,3,128]{3,0,2,1:T(8,128)S(1)} %get-tuple-element.44), channel_id=1, source_target_pairs={{1,0},{2,1},{3,2},{4,3},{5,4},{6,5},{7,6},{8,7},{9,8},{10,9},{11,1... | collective-permute-start | bytes 2359304 | tf_op jit(solution)/shard_map/ppermute | solution.py:28
  124.2 6.9 copy-start.5
  131.1 576.1 %all-to-all-start = ((f32[512,1,5120]{2,1,0:T(1,128)}), f32[512,1,5120]{2,1,0:T(1,128)}, u32[]{:S(2)}, u32[]{:S(2)}) async-start(f32[512,1,5120]{2,1,0:T(1,128)} %stack.54), calls=%async_computation | async-start | bytes 20971520 | tf_op jit(solution)/shard_map/all_to_all | solution.py:174
  152.8 553.4 %all-reduce.24.cloned.1.call-start = ((), (), s32[]{:S(2)}) async-start(), calls=%async_computation.1 | async-start | bytes 131072
  154.7 0.6 copy-start.4
  729.3 8.0 %slice-start = ((s8[10485760]{0:T(1024)(128)(4,1)}), s8[4194304]{0:T(1024)(128)(4,1)S(1)}, s32[]{:S(2)}) async-start(s8[10485760]{0:T(1024)(128)(4,1)} %bitcast.127), calls=%async_computation.2 | async-start | bytes 8388608
  729.3 8.0 %slice-start.1 = ((s8[10485760]{0:T(1024)(128)(4,1)}), s8[2097152]{0:T(1024)(128)(4,1)S(1)}, s32[]{:S(2)}) async-start(s8[10485760]{0:T(1024)(128)(4,1)} %bitcast.127), calls=%async_computation.3 | async-start | bytes 4194304
  734.0 1.3 copy-start.1
  734.0 2.1 copy-start.2
  734.0 3.1 copy-start.3
  734.0 4.5 slice-start.2
Sparse Core Ops, SparseCore 0:
  159.0 547.0 all-reduce.23
